TPU v7x, 256 devices: a whole 4x4x8 slice. The times are simulated.
256 devices in a mesh: scene: 32 (over x, y, core), kd: 8 (over z).
Axes of the slice: x: 4, y: 4, z: 8, core: 2. Of those that a mesh axis runs over, the one named last changes fastest.
Arguments:
- features: bfloat16 [32, 32, 512, 128], P('scene', 'kd'), may hold values from -6 to 6
- send_faces: int32 [32, 8, 3, 1], P('scene', 'kd'), may hold values from 0 to 23, as said below
- face_source: int32 [32, 32, 6], P('scene', 'kd'), may hold values from 0 to 27, as said below
- cotangent: bfloat16 [32, 32, 64, 256], P('scene', 'kd'), may hold values from -12 to 12
- conv_one: bfloat16 [7, 128, 128], replicated, may hold values from -0.1875 to 0.1875
- down_weight: bfloat16 [1024, 256], replicated, may hold values from -0.1875 to 0.1875
- conv_two: bfloat16 [7, 256, 256], replicated, may hold values from -0.125 to 0.125
Outputs:
- encoded: bfloat16 [32, 32, 64, 256], P('scene', 'kd')
- grad_conv_one: float32 [7, 128, 128], replicated
- grad_down: float32 [1024, 256], replicated
- grad_conv_two: float32 [7, 256, 256], replicated
Inputs may be any that keep to these rules, and one draw needn't show every extreme that they name: `send_faces`: entry [i, t] names face 6 b + s of the sender's own brick b; across bit i every device sends exactly one face, of side 2 (i mod 3) + 1 where its bit i is 0 and of side 2 (i mod 3) where it is 1; no face is named twice on a device. `face_source`: for brick b and direction s: a value under 6 * 4 is a local face, of the side opposite s; 24 + i + t is slot t received across bit i; 27 is no neighbour. The relation is symmetric: where direction s of brick b takes a face of brick b2, direction opposite s of b2 takes the face of b at side s, across devices through the same bit and slot.
All inputs are finite; a program needn't handle non-finite values.
Results may differ from a plain program's by a relative error of at most 0.0065.
Values may be sent and summed in bfloat16 or wider, within the bound.
No kernel may reach another device: no remote copies, remote signals or barrier semaphores. Data moves between devices by JAX's collectives and lax.ppermute only.
A program may use at most 64 MiB of HBM per device.

v0:
```python
import jax
import jax.numpy as jnp
from jax import lax
from jax.sharding import PartitionSpec as P

OPPOSITE = (0, 2, 1, 4, 3, 6, 5)


def swapped(value, axis, stride):
    mask = 2**stride
    pairs = [(source, source ^ mask) for source in range(lax.axis_size(axis))]
    return lax.ppermute(value, axis, pairs)


def face_slabs(blocks):
    return jnp.stack(
        [
            blocks[:, 0],
            blocks[:, -1],
            blocks[:, :, 0],
            blocks[:, :, -1],
            blocks[:, :, :, 0],
            blocks[:, :, :, -1],
        ],
        axis=1,
    )


def shift_taps(blocks, border):
    return [
        blocks,
        jnp.concatenate([border[:, 0][:, None], blocks[:, :-1]], 1),
        jnp.concatenate([blocks[:, 1:], border[:, 1][:, None]], 1),
        jnp.concatenate([border[:, 2][:, :, None], blocks[:, :, :-1]], 2),
        jnp.concatenate([blocks[:, :, 1:], border[:, 3][:, :, None]], 2),
        jnp.concatenate([border[:, 4][:, :, :, None], blocks[:, :, :, :-1]], 3),
        jnp.concatenate([blocks[:, :, :, 1:], border[:, 5][:, :, :, None]], 3),
    ]


def conv_apply(taps, weight):
    chans = taps[0].shape[-1]
    total = jnp.dot(taps[0].reshape(-1, chans), weight[0], preferred_element_type=jnp.float32)
    for tap_index in range(1, 7):
        total = total + jnp.dot(
            taps[tap_index].reshape(-1, chans),
            weight[tap_index],
            preferred_element_type=jnp.float32,
        )
    return total


def conv_back(taps, weight):
    chans = taps[0].shape[-1]
    total = lax.dot_general(
        taps[0].reshape(-1, chans),
        weight[0],
        (((1,), (1,)), ((), ())),
        preferred_element_type=jnp.float32,
    )
    for tap_index in range(1, 7):
        total = total + lax.dot_general(
            taps[OPPOSITE[tap_index]].reshape(-1, chans),
            weight[tap_index],
            (((1,), (1,)), ((), ())),
            preferred_element_type=jnp.float32,
        )
    return total


def weight_grads(taps, delta):
    chans = taps[0].shape[-1]
    return jnp.stack(
        [
            lax.dot_general(
                single.reshape(-1, chans),
                delta,
                (((0,), (0,)), ((), ())),
                preferred_element_type=jnp.float32,
            )
            for single in taps
        ]
    )


def down_rows(hidden, brick_count, chans):
    return (
        hidden.reshape(brick_count, 4, 2, 4, 2, 4, 2, chans)
        .transpose(0, 1, 3, 5, 2, 4, 6, 7)
        .reshape(brick_count * 64, 8 * chans)
    )


def up_rows(patch_grad, brick_count, chans):
    return (
        patch_grad.reshape(brick_count, 4, 4, 4, 2, 2, 2, chans)
        .transpose(0, 1, 4, 2, 5, 3, 6, 7)
        .reshape(brick_count * 512, chans)
    )


def silu_slope(value):
    sigma = jax.nn.sigmoid(value)
    return sigma * (1.0 + value * (1.0 - sigma))


def rims_local(blocks, send_list, source_list, swapper):
    brick_count = blocks.shape[0]
    side_cells = blocks.shape[1]
    chans = blocks.shape[-1]
    faces = face_slabs(blocks).reshape(brick_count * 6, side_cells, side_cells, chans)
    pieces = [faces]
    for bit_index in range(send_list.shape[0]):
        pieces.append(swapper(faces[send_list[bit_index]], bit_index))
    pieces.append(jnp.zeros((1, side_cells, side_cells, chans), faces.dtype))
    lookup = jnp.concatenate(pieces, axis=0)
    return lookup[source_list.reshape(-1)].reshape(brick_count, 6, side_cells, side_cells, chans)


def on_device(features, send_faces, face_source, cotangent, conv_one, down_weight, conv_two):
    send_list = send_faces[0, 0]
    source_list = face_source[0]
    brick_count = features.shape[1]
    chan_one = features.shape[3]
    chan_two = cotangent.shape[3]
    grid_one = features[0].reshape(brick_count, 8, 8, 8, chan_one)
    border_one = rims_local(
        grid_one, send_list, source_list, lambda buffer, bit_index: swapped(buffer, "kd", bit_index)
    )
    taps_one = shift_taps(grid_one, border_one)
    pre_one = conv_apply(taps_one, conv_one)
    hidden_one = (
        features[0].reshape(-1, chan_one).astype(jnp.float32) + jax.nn.silu(pre_one)
    ).astype(jnp.bfloat16)
    patches = down_rows(hidden_one, brick_count, chan_one)
    coarse = jnp.dot(patches, down_weight, preferred_element_type=jnp.float32).astype(jnp.bfloat16)
    grid_two = coarse.reshape(brick_count, 4, 4, 4, chan_two)
    border_two = rims_local(
        grid_two, send_list, source_list, lambda buffer, bit_index: swapped(buffer, "kd", bit_index)
    )
    taps_two = shift_taps(grid_two, border_two)
    pre_two = conv_apply(taps_two, conv_two)
    encoded = (coarse.astype(jnp.float32) + jax.nn.silu(pre_two)).astype(jnp.bfloat16)
    upstream = cotangent[0].reshape(-1, chan_two).astype(jnp.float32)
    delta_two = (upstream * silu_slope(pre_two)).astype(jnp.bfloat16)
    grid_delta = delta_two.reshape(brick_count, 4, 4, 4, chan_two)
    border_delta = rims_local(
        grid_delta,
        send_list,
        source_list,
        lambda buffer, bit_index: swapped(buffer, "kd", bit_index),
    )
    taps_delta = shift_taps(grid_delta, border_delta)
    grad_two = weight_grads(taps_two, delta_two)
    grad_coarse = (upstream + conv_back(taps_delta, conv_two)).astype(jnp.bfloat16)
    grad_down = lax.dot_general(
        patches, grad_coarse, (((0,), (0,)), ((), ())), preferred_element_type=jnp.float32
    )
    patch_grad = lax.dot_general(
        grad_coarse, down_weight, (((1,), (1,)), ((), ())), preferred_element_type=jnp.float32
    )
    delta_one = (up_rows(patch_grad, brick_count, chan_one) * silu_slope(pre_one)).astype(
        jnp.bfloat16
    )
    grad_one = weight_grads(taps_one, delta_one)
    grad_one, grad_down, grad_two = lax.psum((grad_one, grad_down, grad_two), ("scene", "kd"))
    return (encoded.reshape(1, brick_count, 64, chan_two), grad_one, grad_down, grad_two)


def solution(mesh):
    placed = (
        P("scene", "kd", None, None),
        P("scene", "kd", None, None),
        P("scene", "kd", None),
        P("scene", "kd", None, None),
        P(),
        P(),
        P(),
    )
    return jax.shard_map(
        on_device,
        mesh=mesh,
        in_specs=placed,
        out_specs=(P("scene", "kd", None, None), P(), P(), P()),
        check_vma=False,
    )
```

profile of v0, /device:TPU:8, one launch (start us, length us, event | category | flops | bytes accessed | tf_op | source)
XLA Modules:
  0.0 421.4 jit_solution(17682841565608177725)
XLA Ops:
  8.2 1.4 fusion.66
  9.6 1.4 fusion.75
  19.4 2.0 collective-permute-start
  21.4 3.3 collective-permute-start.1
  24.7 4.5 %collective-permute-start.2 = (bf16[1,8,8,128]{3,2,1,0:T(8,128)(2,1)S(1)}, bf16[1,8,8,128]{3,2,1,0:T(8,128)(2,1)S(1)}, u32[]{:S(2)}, u32[]{:S(2)}) collective-permute-start(bf16[1,8,8,128]{3,2,1,0:T(8,128)(2,1)S(1)} %get-tuple-element.136), channel_id=1, source_target_pairs={{0,4},{1,5},{2,6},{3,7},{4,0},{5,1},{6,2},{7,3},{8,12},{9,13},{10,... | collective-permute-start | bytes 49160 | tf_op jit(solution)/shard_map/ppermute | solution.py:12
  39.1 1.4 add_convert_fusion
  41.8 1.4 reshape.158
  45.9 1.8 fusion.31
  49.8 1.5 collective-permute-start.4
  51.3 3.8 collective-permute-start.5
  56.2 2.6 collective-permute-done.5
  60.0 1.6 gather_fusion.1
  63.4 1.7 pad_maximum_fusion.7
  66.1 1.7 pad_maximum_fusion.8
  67.8 1.6 reshape.164
  69.3 1.7 pad_maximum_fusion.9
  71.0 1.6 reshape.165
  73.4 1.7 pad_maximum_fusion.10
  75.1 1.6 reshape.166
  77.5 1.7 pad_maximum_fusion.11
  79.2 1.6 reshape.167
  94.4 1.5 collective-permute-start.7
  95.9 3.8 collective-permute-start.8
  100.8 2.6 collective-permute-done.8
  104.6 1.6 gather_fusion.2
  126.0 1.3 fusion.76
  127.3 1.3 fusion.77
  128.6 3.1 reshape.178
  131.8 1.8 copy.159
  140.8 268.1 %all-reduce.3.cloned.1.call-done = (f32[7,128,128]{1,2,0:T(8,128)}, f32[1024,256]{1,0:T(8,128)}, f32[7,256,256]{2,1,0:T(8,128)}) async-done(((f32[7,128,128]{1,2,0:T(8,128)}, f32[1024,256]{1,0:T(8,128)}, f32[7,256,256]{2,1,0:T(8,128)}), (f32[7,128,128]{1,2,0:T(8,128)}, f32[1024,256]{1,0:T(8,128)}, f32[7,256,256]{2,1,0:T(8,128)})) %all-reduce.3.cloned.1.call-update) | async-done | bytes 3342352 | tf_op jit(solution)/shard_map/psum | solution.py:166
  408.9 2.1 copy.166
  411.0 2.3 copy.245
  (200 shorter events, 69.7 us)
Async XLA Ops:
  7.2 36.0 %copy-start = (bf16[1024,256]{1,0:T(8,128)(2,1)S(1)}, bf16[1024,256]{1,0:T(8,128)(2,1)}, u32[]{:S(2)}) copy-start(bf16[1024,256]{1,0:T(8,128)(2,1)} %param.12) | copy-start | bytes 1572868
  7.2 22.0 %copy-start.1 = (bf16[1,4,512,128]{3,2,1,0:T(8,128)(2,1)S(1)}, bf16[1,4,512,128]{3,2,1,0:T(8,128)(2,1)}, u32[]{:S(2)}) copy-start(bf16[1,4,512,128]{3,2,1,0:T(8,128)(2,1)} %param.7) | copy-start | bytes 1572868
  7.2 401.7 %all-reduce.3.cloned.1.call-start = ((), (), s32[]{:S(2)}) async-start(), calls=%async_computation | async-start | bytes 6684672 | tf_op jit(solution)/shard_map/psum | solution.py:166
  19.4 13.6 %collective-permute-start = (bf16[1,8,8,128]{3,2,1,0:T(8,128)(2,1)S(1)}, bf16[1,8,8,128]{3,2,1,0:T(8,128)(2,1)S(1)}, u32[]{:S(2)}, u32[]{:S(2)}) collective-permute-start(bf16[1,8,8,128]{3,2,1,0:T(8,128)(2,1)S(1)} %get-tuple-element.138), channel_id=1, source_target_pairs={{0,1},{1,0},{2,3},{3,2},{4,5},{5,4},{6,7},{7,6},{8,9},{9,8},{10,11... | collective-permute-start | bytes 49160 | tf_op jit(solution)/shard_map/ppermute | solution.py:12
  21.4 11.6 %collective-permute-start.1 = (bf16[1,8,8,128]{3,2,1,0:T(8,128)(2,1)S(1)}, bf16[1,8,8,128]{3,2,1,0:T(8,128)(2,1)S(1)}, u32[]{:S(2)}, u32[]{:S(2)}) collective-permute-start(bf16[1,8,8,128]{3,2,1,0:T(8,128)(2,1)S(1)} %get-tuple-element.137), channel_id=1, source_target_pairs={{0,2},{1,3},{2,0},{3,1},{4,6},{5,7},{6,4},{7,5},{8,10},{9,11},{10,... | collective-permute-start | bytes 49160 | tf_op jit(solution)/shard_map/ppermute | solution.py:12
  24.7 8.4 %collective-permute-start.2 = (bf16[1,8,8,128]{3,2,1,0:T(8,128)(2,1)S(1)}, bf16[1,8,8,128]{3,2,1,0:T(8,128)(2,1)S(1)}, u32[]{:S(2)}, u32[]{:S(2)}) collective-permute-start(bf16[1,8,8,128]{3,2,1,0:T(8,128)(2,1)S(1)} %get-tuple-element.136), channel_id=1, source_target_pairs={{0,4},{1,5},{2,6},{3,7},{4,0},{5,1},{6,2},{7,3},{8,12},{9,13},{10,... | collective-permute-start | bytes 49160 | tf_op jit(solution)/shard_map/ppermute | solution.py:12
  48.0 7.1 %collective-permute-start.3 = (bf16[1,4,4,256]{3,2,1,0:T(4,128)(2,1)S(1)}, bf16[1,4,4,256]{3,2,1,0:T(4,128)(2,1)S(1)}, u32[]{:S(2)}, u32[]{:S(2)}) collective-permute-start(bf16[1,4,4,256]{3,2,1,0:T(4,128)(2,1)S(1)} %get-tuple-element.158), channel_id=1, source_target_pairs={{0,1},{1,0},{2,3},{3,2},{4,5},{5,4},{6,7},{7,6},{8,9},{9,8},{10,11... | collective-permute-start | bytes 24584 | tf_op jit(solution)/shard_map/ppermute | solution.py:12
  49.8 5.8 %collective-permute-start.4 = (bf16[1,4,4,256]{3,2,1,0:T(4,128)(2,1)S(1)}, bf16[1,4,4,256]{3,2,1,0:T(4,128)(2,1)S(1)}, u32[]{:S(2)}, u32[]{:S(2)}) collective-permute-start(bf16[1,4,4,256]{3,2,1,0:T(4,128)(2,1)S(1)} %get-tuple-element.157), channel_id=1, source_target_pairs={{0,2},{1,3},{2,0},{3,1},{4,6},{5,7},{6,4},{7,5},{8,10},{9,11},{10,... | collective-permute-start | bytes 24584 | tf_op jit(solution)/shard_map/ppermute | solution.py:12
  51.3 7.6 %collective-permute-start.5 = (bf16[1,4,4,256]{3,2,1,0:T(4,128)(2,1)S(1)}, bf16[1,4,4,256]{3,2,1,0:T(4,128)(2,1)S(1)}, u32[]{:S(2)}, u32[]{:S(2)}) collective-permute-start(bf16[1,4,4,256]{3,2,1,0:T(4,128)(2,1)S(1)} %get-tuple-element.156), channel_id=1, source_target_pairs={{0,4},{1,5},{2,6},{3,7},{4,0},{5,1},{6,2},{7,3},{8,12},{9,13},{10,... | collective-permute-start | bytes 24584 | tf_op jit(solution)/shard_map/ppermute | solution.py:12
  63.4 18.7 %copy-start.15 = (bf16[256,256]{1,0:T(8,128)(2,1)}, bf16[256,256]{1,0:T(8,128)(2,1)S(1)}, u32[]{:S(2)}) copy-start(bf16[256,256]{1,0:T(8,128)(2,1)S(1)} %reshape.162) | copy-start | bytes 393220
  66.1 17.2 %copy-start.17 = (bf16[256,256]{1,0:T(8,128)(2,1)}, bf16[256,256]{1,0:T(8,128)(2,1)S(1)}, u32[]{:S(2)}) copy-start(bf16[256,256]{1,0:T(8,128)(2,1)S(1)} %reshape.163) | copy-start | bytes 393220
  80.8 3.6 copy-start.6
  80.8 3.6 copy-start.20
  80.8 3.8 copy-start.22
  80.8 4.0 copy-start.26
  80.8 4.0 copy-start.32
  86.8 4.2 copy-start.16
  86.8 4.4 %copy-start.18 = (bf16[256,256]{1,0:T(8,128)(2,1)S(1)}, bf16[256,256]{1,0:T(8,128)(2,1)}, u32[]{:S(2)}) copy-start(bf16[256,256]{1,0:T(8,128)(2,1)} %copy-done.17) | copy-start | bytes 393220
  86.9 4.5 %copy-start.19 = (bf16[256,256]{1,0:T(8,128)(2,1)S(1)}, bf16[256,256]{1,0:T(8,128)(2,1)}, u32[]{:S(2)}) copy-start(bf16[256,256]{1,0:T(8,128)(2,1)} %reshape.164) | copy-start | bytes 393220
  87.7 4.0 copy-start.21
  89.7 9.9 %collective-permute-start.6 = (bf16[1,4,4,256]{3,2,1,0:T(4,128)(2,1)S(1)}, bf16[1,4,4,256]{3,2,1,0:T(4,128)(2,1)S(1)}, u32[]{:S(2)}, u32[]{:S(2)}) collective-permute-start(bf16[1,4,4,256]{3,2,1,0:T(4,128)(2,1)S(1)} %get-tuple-element.149), channel_id=1, source_target_pairs={{0,1},{1,0},{2,3},{3,2},{4,5},{5,4},{6,7},{7,6},{8,9},{9,8},{10,11... | collective-permute-start | bytes 24584 | tf_op jit(solution)/shard_map/ppermute | solution.py:12
  94.4 5.9 %collective-permute-start.7 = (bf16[1,4,4,256]{3,2,1,0:T(4,128)(2,1)S(1)}, bf16[1,4,4,256]{3,2,1,0:T(4,128)(2,1)S(1)}, u32[]{:S(2)}, u32[]{:S(2)}) collective-permute-start(bf16[1,4,4,256]{3,2,1,0:T(4,128)(2,1)S(1)} %get-tuple-element.148), channel_id=1, source_target_pairs={{0,2},{1,3},{2,0},{3,1},{4,6},{5,7},{6,4},{7,5},{8,10},{9,11},{10,... | collective-permute-start | bytes 24584 | tf_op jit(solution)/shard_map/ppermute | solution.py:12
  95.9 7.6 %collective-permute-start.8 = (bf16[1,4,4,256]{3,2,1,0:T(4,128)(2,1)S(1)}, bf16[1,4,4,256]{3,2,1,0:T(4,128)(2,1)S(1)}, u32[]{:S(2)}, u32[]{:S(2)}) collective-permute-start(bf16[1,4,4,256]{3,2,1,0:T(4,128)(2,1)S(1)} %get-tuple-element.147), channel_id=1, source_target_pairs={{0,4},{1,5},{2,6},{3,7},{4,0},{5,1},{6,2},{7,3},{8,12},{9,13},{10,... | collective-permute-start | bytes 24584 | tf_op jit(solution)/shard_map/ppermute | solution.py:12
  107.0 11.9 %copy-start.24 = (f32[256,256]{1,0:T(8,128)S(1)}, f32[256,256]{1,0:T(8,128)}, u32[]{:S(2)}) copy-start(f32[256,256]{1,0:T(8,128)} %fusion.29) | copy-start | bytes 786436
  118.8 3.7 copy-start.28
  118.9 4.8 %copy-start.29 = (bf16[256,256]{1,0:T(8,128)(2,1)S(1)}, bf16[256,256]{1,0:T(8,128)(2,1)}, u32[]{:S(2)}) copy-start(bf16[256,256]{1,0:T(8,128)(2,1)} %reshape.176) | copy-start | bytes 393220
  118.9 6.0 %copy-start.30 = (bf16[256,256]{1,0:T(8,128)(2,1)S(1)}, bf16[256,256]{1,0:T(8,128)(2,1)}, u32[]{:S(2)}) copy-start(bf16[256,256]{1,0:T(8,128)(2,1)} %reshape.177) | copy-start | bytes 393220
  118.9 6.0 %copy-start.33 = (bf16[1,4,64,256]{3,2,1,0:T(8,128)(2,1)S(1)}, bf16[1,4,64,256]{3,2,1,0:T(8,128)(2,1)}, u32[]{:S(2)}) copy-start(bf16[1,4,64,256]{3,2,1,0:T(8,128)(2,1)} %param.10) | copy-start | bytes 393220
  134.0 2.9 copy-start.3
  135.9 2.9 copy-start.5
  136.9 2.9 copy-start.9
  408.9 4.4 %copy-start.12 = (f32[7,256,256]{2,1,0:T(8,128)S(1)}, f32[7,256,256]{2,1,0:T(8,128)}, u32[]{:S(2)}) copy-start(f32[7,256,256]{2,1,0:T(8,128)} %get-tuple-element.189) | copy-start | bytes 5505028
  (13 other events, 21.7 us)
Sparse Core Ops, SparseCore 0:
  141.0 267.9 all-reduce.2
where the time goes:
time: 423 us; the launch traced here: 421 us
  waiting for transfers between devices  273 us (65%)
  local copies, waits for them, and re-layouts  57.9 us (14%)
  matrix products  29.1 us (7%)
  starting transfers between devices  22.6 us (5%)
  between operations  20.7 us (5%)
  other arithmetic  17.8 us (4%)
    psum x1, waiting for transfers between devices, on_device(): lax.psum((grad_one, grad_down, grad_two), ('scene', 'kd'))  268 us
    ppermute x9, starting transfers between devices, swapped(): return lax.ppermute(value, axis, pairs)  22.6 us
    unnamed x100, local copies, waits for them, and re-layouts  17.6 us
  transfers between devices with their start and end apart: 10, of which 3 were waited for; matrix products, arithmetic and copies ran while one was open for 2% of the time, Pallas kernels for 0%

commit v1 on v0

--- a/solution.py
+++ b/solution.py
@@ -163,7 +163,9 @@
         jnp.bfloat16
     )
     grad_one = weight_grads(taps_one, delta_one)
-    grad_one, grad_down, grad_two = lax.psum((grad_one, grad_down, grad_two), ("scene", "kd"))
+    grad_one, grad_down, grad_two = lax.psum(
+        lax.psum((grad_one, grad_down, grad_two), "scene"), "kd"
+    )
     return (encoded.reshape(1, brick_count, 64, chan_two), grad_one, grad_down, grad_two)
 
 

time: 423 us -> 368 us (0.87)
  waiting for transfers between devices: 273 us -> 222 us
    psum x1 -> x2, waiting for transfers between devices: 268 us -> 216 us  [the longest x1 118 us: on_device(): lax.psum((grad_one, grad_down, grad_two), 'scene')]
    dot_general x14, matrix products: 8.38 us -> 3.99 us  [weight_grads(): lax.dot_general(single.reshape(-1, chans), delta, (((0,), (0,)), ((), ())...]
    unnamed x100 -> x102, local copies, waits for them, and re-layouts: 17.6 us -> 18.2 us
  transfers between devices with their start and end apart: 10 -> 11, of which waited for: 3 -> 4; matrix products, arithmetic and copies ran while one was open for 2% -> 3% of each run, Pallas kernels for 0% -> 0%
where the time goes in v1:
time: 368 us; the launch traced here: 366 us
  waiting for transfers between devices  222 us (60%)
  local copies, waits for them, and re-layouts  58.2 us (16%)
  matrix products  25.7 us (7%)
  starting transfers between devices  21.3 us (6%)
  between operations  20.8 us (6%)
  other arithmetic  17.7 us (5%)
    psum x1, waiting for transfers between devices, on_device(): lax.psum((grad_one, grad_down, grad_two), 'scene')  118 us
    psum x1, waiting for transfers between devices, on_device(): lax.psum(lax.psum((grad_one, grad_down, grad_two), 'scene'), 'kd')  97.4 us
    ppermute x9, starting transfers between devices, swapped(): return lax.ppermute(value, axis, pairs)  21.2 us
    unnamed x102, local copies, waits for them, and re-layouts  18.2 us
    dot_general x12, matrix products, conv_apply(): jnp.dot(taps[tap_index].reshape(-1, chans), weight[tap_index], preferred_...  7.73 us
  transfers between devices with their start and end apart: 11, of which 4 were waited for; matrix products, arithmetic and copies ran while one was open for 3% of the time, Pallas kernels for 0%

profile of v1, /device:TPU:8, one launch (start us, length us, event | category | flops | bytes accessed | tf_op | source)
XLA Modules:
  0.0 365.8 jit_solution(17991512009416223425)
XLA Ops:
  8.2 1.4 fusion.66
  9.6 1.4 fusion.75
  19.4 2.0 collective-permute-start
  21.4 3.3 collective-permute-start.1
  24.7 4.5 %collective-permute-start.2 = (bf16[1,8,8,128]{3,2,1,0:T(8,128)(2,1)S(1)}, bf16[1,8,8,128]{3,2,1,0:T(8,128)(2,1)S(1)}, u32[]{:S(2)}, u32[]{:S(2)}) collective-permute-start(bf16[1,8,8,128]{3,2,1,0:T(8,128)(2,1)S(1)} %get-tuple-element.139), channel_id=1, source_target_pairs={{0,4},{1,5},{2,6},{3,7},{4,0},{5,1},{6,2},{7,3},{8,12},{9,13},{10,... | collective-permute-start | bytes 49160 | tf_op jit(solution)/shard_map/ppermute | solution.py:12
  39.6 1.4 add_convert_fusion
  42.3 1.4 reshape.158
  46.4 1.8 fusion.31
  50.2 1.5 collective-permute-start.4
  51.7 3.1 collective-permute-start.5
  56.0 3.3 collective-permute-done.5
  60.5 1.6 gather_fusion.1
  63.9 1.7 pad_maximum_fusion.7
  66.5 1.7 pad_maximum_fusion.8
  68.2 1.6 reshape.164
  69.8 1.7 pad_maximum_fusion.9
  71.5 1.6 reshape.165
  73.9 1.7 pad_maximum_fusion.10
  75.6 1.6 reshape.166
  78.0 1.7 pad_maximum_fusion.11
  79.7 1.6 reshape.167
  94.8 1.5 collective-permute-start.7
  96.3 3.1 collective-permute-start.8
  100.6 3.3 collective-permute-done.8
  105.1 1.6 gather_fusion.2
  126.4 1.4 fusion.76
  129.1 3.1 reshape.178
  132.2 1.8 copy.159
  137.8 118.2 %all-reduce.5.cloned.1.call-done = (f32[7,128,128]{1,2,0:T(8,128)}, f32[1024,256]{1,0:T(8,128)}, f32[7,256,256]{2,1,0:T(8,128)}) async-done(((f32[7,128,128]{1,2,0:T(8,128)}, f32[1024,256]{1,0:T(8,128)}, f32[7,256,256]{2,1,0:T(8,128)}), (f32[7,128,128]{1,2,0:T(8,128)}, f32[1024,256]{1,0:T(8,128)}, f32[7,256,256]{2,1,0:T(8,128)})) %all-reduce.5.cloned.1.call-update) | async-done | bytes 3342352 | tf_op jit(solution)/shard_map/psum | solution.py:167
  255.9 97.4 %all-reduce.7.cloned.1.call-done = (f32[7,128,128]{1,2,0:T(8,128)}, f32[1024,256]{1,0:T(8,128)}, f32[7,256,256]{2,1,0:T(8,128)}) async-done(((f32[7,128,128]{1,2,0:T(8,128)}, f32[1024,256]{1,0:T(8,128)}, f32[7,256,256]{2,1,0:T(8,128)}), (f32[7,128,128]{1,2,0:T(8,128)}, f32[1024,256]{1,0:T(8,128)}, f32[7,256,256]{2,1,0:T(8,128)})) %all-reduce.7.cloned.1.call-update) | async-done | bytes 3342352 | tf_op jit(solution)/shard_map/psum | solution.py:166
  353.4 2.1 copy.166
  355.5 2.3 copy.248
  (205 shorter events, 67.9 us)
Async XLA Ops:
  7.2 36.5 %copy-start = (bf16[1024,256]{1,0:T(8,128)(2,1)S(1)}, bf16[1024,256]{1,0:T(8,128)(2,1)}, u32[]{:S(2)}) copy-start(bf16[1024,256]{1,0:T(8,128)(2,1)} %param.12) | copy-start | bytes 1572868
  7.2 22.0 %copy-start.1 = (bf16[1,4,512,128]{3,2,1,0:T(8,128)(2,1)S(1)}, bf16[1,4,512,128]{3,2,1,0:T(8,128)(2,1)}, u32[]{:S(2)}) copy-start(bf16[1,4,512,128]{3,2,1,0:T(8,128)(2,1)} %param.7) | copy-start | bytes 1572868
  7.2 248.7 %all-reduce.5.cloned.1.call-start = ((), (), s32[]{:S(2)}) async-start(), calls=%async_computation | async-start | bytes 6684672 | tf_op jit(solution)/shard_map/psum | solution.py:167
  19.4 14.3 %collective-permute-start = (bf16[1,8,8,128]{3,2,1,0:T(8,128)(2,1)S(1)}, bf16[1,8,8,128]{3,2,1,0:T(8,128)(2,1)S(1)}, u32[]{:S(2)}, u32[]{:S(2)}) collective-permute-start(bf16[1,8,8,128]{3,2,1,0:T(8,128)(2,1)S(1)} %get-tuple-element.141), channel_id=1, source_target_pairs={{0,1},{1,0},{2,3},{3,2},{4,5},{5,4},{6,7},{7,6},{8,9},{9,8},{10,11... | collective-permute-start | bytes 49160 | tf_op jit(solution)/shard_map/ppermute | solution.py:12
  21.4 12.3 %collective-permute-start.1 = (bf16[1,8,8,128]{3,2,1,0:T(8,128)(2,1)S(1)}, bf16[1,8,8,128]{3,2,1,0:T(8,128)(2,1)S(1)}, u32[]{:S(2)}, u32[]{:S(2)}) collective-permute-start(bf16[1,8,8,128]{3,2,1,0:T(8,128)(2,1)S(1)} %get-tuple-element.140), channel_id=1, source_target_pairs={{0,2},{1,3},{2,0},{3,1},{4,6},{5,7},{6,4},{7,5},{8,10},{9,11},{10,... | collective-permute-start | bytes 49160 | tf_op jit(solution)/shard_map/ppermute | solution.py:12
  24.7 9.0 %collective-permute-start.2 = (bf16[1,8,8,128]{3,2,1,0:T(8,128)(2,1)S(1)}, bf16[1,8,8,128]{3,2,1,0:T(8,128)(2,1)S(1)}, u32[]{:S(2)}, u32[]{:S(2)}) collective-permute-start(bf16[1,8,8,128]{3,2,1,0:T(8,128)(2,1)S(1)} %get-tuple-element.139), channel_id=1, source_target_pairs={{0,4},{1,5},{2,6},{3,7},{4,0},{5,1},{6,2},{7,3},{8,12},{9,13},{10,... | collective-permute-start | bytes 49160 | tf_op jit(solution)/shard_map/ppermute | solution.py:12
  48.4 6.4 %collective-permute-start.3 = (bf16[1,4,4,256]{3,2,1,0:T(4,128)(2,1)S(1)}, bf16[1,4,4,256]{3,2,1,0:T(4,128)(2,1)S(1)}, u32[]{:S(2)}, u32[]{:S(2)}) collective-permute-start(bf16[1,4,4,256]{3,2,1,0:T(4,128)(2,1)S(1)} %get-tuple-element.161), channel_id=1, source_target_pairs={{0,1},{1,0},{2,3},{3,2},{4,5},{5,4},{6,7},{7,6},{8,9},{9,8},{10,11... | collective-permute-start | bytes 24584 | tf_op jit(solution)/shard_map/ppermute | solution.py:12
  50.2 5.2 %collective-permute-start.4 = (bf16[1,4,4,256]{3,2,1,0:T(4,128)(2,1)S(1)}, bf16[1,4,4,256]{3,2,1,0:T(4,128)(2,1)S(1)}, u32[]{:S(2)}, u32[]{:S(2)}) collective-permute-start(bf16[1,4,4,256]{3,2,1,0:T(4,128)(2,1)S(1)} %get-tuple-element.160), channel_id=1, source_target_pairs={{0,2},{1,3},{2,0},{3,1},{4,6},{5,7},{6,4},{7,5},{8,10},{9,11},{10,... | collective-permute-start | bytes 24584 | tf_op jit(solution)/shard_map/ppermute | solution.py:12
  51.7 7.6 %collective-permute-start.5 = (bf16[1,4,4,256]{3,2,1,0:T(4,128)(2,1)S(1)}, bf16[1,4,4,256]{3,2,1,0:T(4,128)(2,1)S(1)}, u32[]{:S(2)}, u32[]{:S(2)}) collective-permute-start(bf16[1,4,4,256]{3,2,1,0:T(4,128)(2,1)S(1)} %get-tuple-element.159), channel_id=1, source_target_pairs={{0,4},{1,5},{2,6},{3,7},{4,0},{5,1},{6,2},{7,3},{8,12},{9,13},{10,... | collective-permute-start | bytes 24584 | tf_op jit(solution)/shard_map/ppermute | solution.py:12
  63.8 18.7 %copy-start.15 = (bf16[256,256]{1,0:T(8,128)(2,1)}, bf16[256,256]{1,0:T(8,128)(2,1)S(1)}, u32[]{:S(2)}) copy-start(bf16[256,256]{1,0:T(8,128)(2,1)S(1)} %reshape.162) | copy-start | bytes 393220
  66.5 17.2 %copy-start.17 = (bf16[256,256]{1,0:T(8,128)(2,1)}, bf16[256,256]{1,0:T(8,128)(2,1)S(1)}, u32[]{:S(2)}) copy-start(bf16[256,256]{1,0:T(8,128)(2,1)S(1)} %reshape.163) | copy-start | bytes 393220
  81.3 3.6 copy-start.7
  81.3 3.6 copy-start.20
  81.3 3.8 %copy-start.22 = (bf16[256,256]{1,0:T(8,128)(2,1)S(1)}, bf16[256,256]{1,0:T(8,128)(2,1)}, u32[]{:S(2)}) copy-start(bf16[256,256]{1,0:T(8,128)(2,1)} %reshape.166) | copy-start | bytes 393220
  81.3 4.0 %copy-start.27 = (bf16[256,256]{1,0:T(8,128)(2,1)S(1)}, bf16[256,256]{1,0:T(8,128)(2,1)}, u32[]{:S(2)}) copy-start(bf16[256,256]{1,0:T(8,128)(2,1)} %reshape.167) | copy-start | bytes 393220
  81.3 4.0 %copy-start.33 = (bf16[1,4,64,256]{3,2,1,0:T(8,128)(2,1)S(1)}, bf16[1,4,64,256]{3,2,1,0:T(8,128)(2,1)}, u32[]{:S(2)}) copy-start(bf16[1,4,64,256]{3,2,1,0:T(8,128)(2,1)} %param.10) | copy-start | bytes 393220
  87.2 4.2 %copy-start.16 = (bf16[256,256]{1,0:T(8,128)(2,1)S(1)}, bf16[256,256]{1,0:T(8,128)(2,1)}, u32[]{:S(2)}) copy-start(bf16[256,256]{1,0:T(8,128)(2,1)} %copy-done.15) | copy-start | bytes 393220
  87.3 4.4 %copy-start.18 = (bf16[256,256]{1,0:T(8,128)(2,1)S(1)}, bf16[256,256]{1,0:T(8,128)(2,1)}, u32[]{:S(2)}) copy-start(bf16[256,256]{1,0:T(8,128)(2,1)} %copy-done.17) | copy-start | bytes 393220
  87.4 4.5 %copy-start.19 = (bf16[256,256]{1,0:T(8,128)(2,1)S(1)}, bf16[256,256]{1,0:T(8,128)(2,1)}, u32[]{:S(2)}) copy-start(bf16[256,256]{1,0:T(8,128)(2,1)} %reshape.164) | copy-start | bytes 393220
  88.2 4.0 %copy-start.21 = (bf16[256,256]{1,0:T(8,128)(2,1)S(1)}, bf16[256,256]{1,0:T(8,128)(2,1)}, u32[]{:S(2)}) copy-start(bf16[256,256]{1,0:T(8,128)(2,1)} %reshape.165) | copy-start | bytes 393220
  89.7 2.7 copy-start.23
  89.9 2.7 copy-start.28
  90.2 9.3 %collective-permute-start.6 = (bf16[1,4,4,256]{3,2,1,0:T(4,128)(2,1)S(1)}, bf16[1,4,4,256]{3,2,1,0:T(4,128)(2,1)S(1)}, u32[]{:S(2)}, u32[]{:S(2)}) collective-permute-start(bf16[1,4,4,256]{3,2,1,0:T(4,128)(2,1)S(1)} %get-tuple-element.152), channel_id=1, source_target_pairs={{0,1},{1,0},{2,3},{3,2},{4,5},{5,4},{6,7},{7,6},{8,9},{9,8},{10,11... | collective-permute-start | bytes 24584 | tf_op jit(solution)/shard_map/ppermute | solution.py:12
  94.8 5.2 %collective-permute-start.7 = (bf16[1,4,4,256]{3,2,1,0:T(4,128)(2,1)S(1)}, bf16[1,4,4,256]{3,2,1,0:T(4,128)(2,1)S(1)}, u32[]{:S(2)}, u32[]{:S(2)}) collective-permute-start(bf16[1,4,4,256]{3,2,1,0:T(4,128)(2,1)S(1)} %get-tuple-element.151), channel_id=1, source_target_pairs={{0,2},{1,3},{2,0},{3,1},{4,6},{5,7},{6,4},{7,5},{8,10},{9,11},{10,... | collective-permute-start | bytes 24584 | tf_op jit(solution)/shard_map/ppermute | solution.py:12
  96.3 7.6 %collective-permute-start.8 = (bf16[1,4,4,256]{3,2,1,0:T(4,128)(2,1)S(1)}, bf16[1,4,4,256]{3,2,1,0:T(4,128)(2,1)S(1)}, u32[]{:S(2)}, u32[]{:S(2)}) collective-permute-start(bf16[1,4,4,256]{3,2,1,0:T(4,128)(2,1)S(1)} %get-tuple-element.150), channel_id=1, source_target_pairs={{0,4},{1,5},{2,6},{3,7},{4,0},{5,1},{6,2},{7,3},{8,12},{9,13},{10,... | collective-permute-start | bytes 24584 | tf_op jit(solution)/shard_map/ppermute | solution.py:12
  107.4 11.9 %copy-start.24 = (f32[256,256]{1,0:T(8,128)S(1)}, f32[256,256]{1,0:T(8,128)}, u32[]{:S(2)}) copy-start(f32[256,256]{1,0:T(8,128)} %fusion.29) | copy-start | bytes 786436
  119.3 3.7 %copy-start.29 = (bf16[256,256]{1,0:T(8,128)(2,1)S(1)}, bf16[256,256]{1,0:T(8,128)(2,1)}, u32[]{:S(2)}) copy-start(bf16[256,256]{1,0:T(8,128)(2,1)} %reshape.175) | copy-start | bytes 393220
  119.3 4.8 %copy-start.30 = (bf16[256,256]{1,0:T(8,128)(2,1)S(1)}, bf16[256,256]{1,0:T(8,128)(2,1)}, u32[]{:S(2)}) copy-start(bf16[256,256]{1,0:T(8,128)(2,1)} %reshape.176) | copy-start | bytes 393220
  119.3 6.0 %copy-start.31 = (bf16[256,256]{1,0:T(8,128)(2,1)S(1)}, bf16[256,256]{1,0:T(8,128)(2,1)}, u32[]{:S(2)}) copy-start(bf16[256,256]{1,0:T(8,128)(2,1)} %reshape.177) | copy-start | bytes 393220
  119.3 6.0 %copy-start.34 = (bf16[1,4,64,256]{3,2,1,0:T(8,128)(2,1)S(1)}, bf16[1,4,64,256]{3,2,1,0:T(8,128)(2,1)}, u32[]{:S(2)}) copy-start(bf16[1,4,64,256]{3,2,1,0:T(8,128)(2,1)} %param.10) | copy-start | bytes 393220
  137.7 215.7 %all-reduce.7.cloned.1.call-start = ((), (), s32[]{:S(2)}) async-start(), calls=%async_computation.1 | async-start | bytes 6684672 | tf_op jit(solution)/shard_map/psum | solution.py:166
  353.4 4.4 %copy-start.12 = (f32[7,256,256]{2,1,0:T(8,128)S(1)}, f32[7,256,256]{2,1,0:T(8,128)}, u32[]{:S(2)}) copy-start(f32[7,256,256]{2,1,0:T(8,128)} %get-tuple-element.192) | copy-start | bytes 5505028
  (15 other events, 20.4 us)
Sparse Core Ops, SparseCore 0:
  137.8 118.0 all-reduce.4
  258.5 94.8 all-reduce.6
